TPU v7x, 32 devices: a whole 2x2x4 slice. The times are simulated.
32 devices in a mesh: parts: 2 (over y), pool: 4 (over z), tp: 4 (over x, core).
Axes of the slice: x: 2, y: 2, z: 4, core: 2. Of those that a mesh axis runs over, the one named last changes fastest.
Arguments:
- queries: bfloat16 [4096, 8192], P(('parts', 'pool'), 'tp'), parts along dimension 0, may hold values from -400 to 400
- suffix_kv: bfloat16 [2, 8, 4096, 128], P(None, 'tp', ('parts', 'pool')), parts along dimension 2, may hold values from -12 to 12
- pool_kv: bfloat16 [2, 8, 64, 128, 128], P(None, 'tp', ('parts', 'pool')), parts along dimension 2, may hold values from -6 to 6
- prefix_pages: int32 [8], P('parts'), parts along dimension 0, may hold values from 1 to 4, as said below
- owner_start: int32 [8], P('parts'), parts along dimension 0, may hold values from 0 to 3
- page_slot: int32 [8, 4, 2], P('parts'), parts along dimension 0, may hold values from 0 to 7, as said below
Outputs:
- attention: bfloat16 [4096, 8192], P(('parts', 'pool'), 'tp'), parts along dimension 0
- new_pool: bfloat16 [2, 8, 64, 128, 128], P(None, 'tp', ('parts', 'pool')), parts along dimension 2
There are 2 independent parts, one for each index of `parts`. A program takes and returns all parts, laid end to end along the dimension named above; each array names one. Nothing has to cross between parts.
Inputs may be any that keep to these rules, and one draw needn't show every extreme that they name: For each owner o, the entries page_slot[:, o, :] name each of its 8 slots exactly once. `prefix_pages`: among the 4 requests of one serving group, at least one has exactly 4 prefix pages.
All inputs are finite; a program needn't handle non-finite values.
Results may differ from a plain program's by a relative error of at most 0.0035.
Values may be sent and summed in bfloat16 or wider, within the bound.
A program may use at most 128 MiB of HBM per device.

v0:
```python
import math
import jax
import jax.numpy as jnp
from jax import lax
from jax.sharding import PartitionSpec as P


def attend_block(running, query_heads, key_rows, value_rows, visible, score_scale):
    run_max, weight_sum, accumulated = running
    scores = (
        jnp.einsum("hgqd,hkd->hgqk", query_heads, key_rows, preferred_element_type=jnp.float32)
        * score_scale
    )
    scores = jnp.where(visible, scores, -jnp.inf)
    new_max = jnp.maximum(run_max, jnp.max(scores, axis=-1))
    factor = jnp.exp(run_max - new_max)
    weights = jnp.exp(scores - new_max[..., None])
    weight_sum = weight_sum * factor + jnp.sum(weights, axis=-1)
    accumulated = accumulated * factor[..., None] + jnp.einsum(
        "hgqk,hkd->hgqd",
        weights.astype(jnp.bfloat16),
        value_rows,
        preferred_element_type=jnp.float32,
    )
    return (new_max, weight_sum, accumulated)


def attend_pages(running, query_heads, received, numbers, length, score_scale):
    page_count = received.shape[2]
    page_len = received.shape[3]
    per_block = min(page_count, max(1, 512 // page_len))
    while page_count % per_block:
        per_block = per_block - 1

    def block_step(block_index, carried):
        block_start = block_index * per_block
        block_pages = lax.dynamic_slice_in_dim(received, block_start, per_block, 2)
        key_rows = block_pages[0].reshape(
            block_pages.shape[1], per_block * page_len, block_pages.shape[4]
        )
        value_rows = block_pages[1].reshape(
            block_pages.shape[1], per_block * page_len, block_pages.shape[4]
        )
        live_pages = lax.dynamic_slice_in_dim(numbers, block_start, per_block, 0) < length
        visible = jnp.repeat(live_pages, page_len)
        return attend_block(carried, query_heads, key_rows, value_rows, visible, score_scale)

    return lax.fori_loop(0, page_count // per_block, block_step, running)


def body(queries, suffix_kv, pool_kv, prefix_pages, owner_start, page_slot):
    groups = lax.axis_size("pool")
    my_index = lax.axis_index("pool")
    local_heads = pool_kv.shape[1]
    slot_count = pool_kv.shape[2]
    page_len = pool_kv.shape[3]
    head_dim = pool_kv.shape[4]
    levels = page_slot.shape[2]
    suffix = queries.shape[0]
    per_kv = queries.shape[1] // (local_heads * head_dim)
    suffix_pages = suffix // page_len
    score_scale = 1.0 / math.sqrt(head_dim)
    length = prefix_pages[my_index]
    start_owner = owner_start[my_index]
    owners = jnp.arange(groups, dtype=jnp.int32)
    my_slots = page_slot[:, my_index, :]

    def level_rows(begin_level, end_level):
        chosen = my_slots[:, begin_level:end_level].reshape(-1)
        return jnp.take(pool_kv, chosen, axis=2)

    def numbers_of(begin_level, end_level):
        within = jnp.mod(owners - start_owner, groups)
        level_ids = jnp.arange(begin_level, end_level, dtype=jnp.int32)
        return (level_ids[None, :] * groups + within[:, None]).reshape(-1)

    own_pages = suffix_kv.reshape(2, local_heads, suffix_pages, page_len, head_dim)
    offset = jnp.mod(owners - start_owner - length, groups)
    wanted = offset < suffix_pages
    picked = jnp.take(own_pages, jnp.minimum(offset, suffix_pages - 1), axis=2)
    back_send = jnp.where(wanted[None, None, :, None, None], picked, jnp.zeros_like(picked))
    level_spans = [(level_one, level_one + 1) for level_one in range(levels)]
    first_send = level_rows(level_spans[0][0], level_spans[0][1])
    first_recv = lax.all_to_all(first_send, "pool", split_axis=2, concat_axis=2, tiled=True)
    returned = lax.all_to_all(back_send, "pool", split_axis=2, concat_axis=2, tiled=True)
    query_heads = jnp.transpose(
        queries.reshape(suffix, local_heads, per_kv, head_dim), (1, 2, 0, 3)
    )
    causal = lax.broadcasted_iota(jnp.int32, (suffix, suffix), 1) <= lax.broadcasted_iota(
        jnp.int32, (suffix, suffix), 0
    )
    running = (
        jnp.full((local_heads, per_kv, suffix), -jnp.inf, jnp.float32),
        jnp.zeros((local_heads, per_kv, suffix), jnp.float32),
        jnp.zeros((local_heads, per_kv, suffix, head_dim), jnp.float32),
    )
    running = attend_block(running, query_heads, suffix_kv[0], suffix_kv[1], causal, score_scale)
    running = attend_pages(
        running,
        query_heads,
        first_recv,
        numbers_of(level_spans[0][0], level_spans[0][1]),
        length,
        score_scale,
    )
    for begin_level, end_level in level_spans[1:]:
        later_recv = lax.all_to_all(
            level_rows(begin_level, end_level), "pool", split_axis=2, concat_axis=2, tiled=True
        )
        running = attend_pages(
            running,
            query_heads,
            later_recv,
            numbers_of(begin_level, end_level),
            length,
            score_scale,
        )
    run_max, weight_sum, accumulated = running
    result = accumulated / weight_sum[..., None]
    result = (
        jnp.transpose(result, (2, 0, 1, 3))
        .reshape(suffix, local_heads * per_kv * head_dim)
        .astype(jnp.bfloat16)
    )
    offset_in = jnp.mod(my_index - owner_start - prefix_pages, groups)
    usable = offset_in < suffix_pages
    level_ids = jnp.minimum((prefix_pages + offset_in) // groups, levels - 1)
    target = jnp.take_along_axis(my_slots, level_ids[:, None], axis=1)[:, 0]
    target = jnp.where(usable, target, slot_count)
    new_pool = pool_kv.at[:, :, target].set(returned, mode="drop")
    return (result, new_pool)


def solution(mesh):
    in_specs = (
        P(("parts", "pool"), "tp"),
        P(None, "tp", ("parts", "pool"), None),
        P(None, "tp", ("parts", "pool"), None, None),
        P("parts"),
        P("parts"),
        P("parts", None, None),
    )
    out_specs = (P(("parts", "pool"), "tp"), P(None, "tp", ("parts", "pool"), None, None))
    return jax.shard_map(body, mesh=mesh, in_specs=in_specs, out_specs=out_specs, check_vma=False)
```

profile of v0, /device:TPU:0, one launch (start us, length us, event | category | flops | bytes accessed | tf_op | source)
XLA Modules:
  0.0 122.8 jit_solution(5285862944854950834)
XLA Ops:
  0.6 0.0 copy-start
  0.6 1.2 %copy.61 = bf16[2,2,8,128,128]{4,3,2,1,0:T(8,128)(2,1)S(1)} copy(bf16[2,2,8,128,128]{4,3,2,1,0:T(8,128)(2,1)} %param.10) | data formatting | bytes 2097152
  1.9 0.0 copy-done
  1.9 0.1 constant_dynamic-slice_fusion
  2.0 0.1 copy.22
  2.1 0.6 gather_fusion.2
  2.7 0.9 select_bitcast_fusion.1
  3.6 6.3 %all-to-all-start = ((bf16[2,2,4,128,128]{4,3,1,0,2:T(8,128)(2,1)}), bf16[2,2,4,128,128]{4,3,1,0,2:T(8,128)(2,1)}, u32[]{:S(2)}, u32[]{:S(2)}) async-start(bf16[2,2,4,128,128]{4,3,1,0,2:T(8,128)(2,1)} %select_bitcast_fusion.1), calls=%async_computation | async-start | bytes 1048576 | tf_op jit(solution)/shard_map/all_to_all | solution.py:84
  10.0 1.3 %dynamic_slice.17 = s32[1]{0:T(128)} dynamic-slice(s32[4]{0:T(128)} %param.12, s32[]{:T(128)S(6)} %select_n.118), dynamic_slice_sizes={1} | dynamic-slice | bytes 12 | tf_op jit(solution)/shard_map/dynamic_slice | solution.py:64
  11.3 1.2 %dynamic_slice.18 = s32[1]{0:T(128)} dynamic-slice(s32[4]{0:T(128)} %param.11, s32[]{:T(128)S(6)} %select_n.118), dynamic_slice_sizes={1} | dynamic-slice | bytes 12 | tf_op jit(solution)/shard_map/dynamic_slice | solution.py:63
  12.5 0.7 compare_select_fusion.5
  13.2 1.2 fusion.50
  14.4 1.2 add_compare_fusion
  15.6 0.1 iota_compare_fusion
  15.7 0.1 broadcast_bitcast_fusion
  15.8 0.1 broadcast_bitcast_fusion.1
  15.9 0.6 gather_fusion.1
  16.5 1.4 %gather_fusion.3 = bf16[4,2,2,128,128]{4,3,2,1,0:T(8,128)(2,1)} fusion(bf16[2,2,8,128,128]{4,3,2,1,0:T(8,128)(2,1)S(1)} %copy.61, s32[1024]{0:T(1024)S(1)} %pad_clamp_fusion.1), kind=kCustom, calls=%fused_computation.1.clone | custom fusion | bytes 1048592 | tf_op jit(solution)/shard_map/jit(_take)/gather | solution.py:70
  17.9 2.2 %copy.40 = bf16[64,8,16,128]{3,2,1,0:T(8,128)(2,1)S(1)} copy(bf16[64,8,16,128]{3,1,2,0:T(8,128)(2,1)} %bitcast.169) | data formatting | bytes 4194304
  20.1 2.5 %gather_fusion = bf16[4,2,2,128,128]{4,3,2,1,0:T(8,128)(2,1)} fusion(bf16[2,2,4,128,128]{4,3,2,1,0:T(8,128)(2,1)} %bitcast.171, s32[1024]{0:T(1024)S(1)} %pad_clamp_fusion), kind=kCustom, calls=%fused_computation.2 | custom fusion | bytes 1048592 | tf_op jit(solution)/shard_map/jit(_take)/gather | solution.py:80
  22.6 1.9 %select_bitcast_fusion = bf16[2,2,4,128,128]{4,3,1,0,2:T(8,128)(2,1)} fusion(bf16[4,2,2,128,128]{4,3,2,1,0:T(8,128)(2,1)} %gather_fusion.3, pred[4]{0:T(512)(128)(4,1)S(1)} %get-tuple-element.77), kind=kLoop, calls=%fused_computation.45 | loop fusion | flops 262144 | bytes 1048580 | tf_op jit(solution)/shard_map/jit(_take)/select_n | solution.py:70
  24.6 8.3 %fusion.2 = (f32[2,8,512]{2,1,0:T(8,128)S(1)}, f32[2,8,512,512]{2,3,1,0:T(8,128)}) fusion(pred[512,512]{0,1:T(8,128)(4,1)S(1)} %iota_compare_fusion, bf16[2,2,512,128]{3,2,1,0:T(8,128)(2,1)} %param.9, bf16[512,2,8,128]{3,2,1,0:T(8,128)(2,1)S(1)} %bitcast.166), kind=kOutput, calls=%fused_computation.15 | convolution fusion | flops 1086316544 | bytes 19431424 | tf_op jit(solution)/shard_map/hgqd,hkd->hgqk/dot_general | solution.py:11
  32.8 9.4 %fusion.3 = f32[2,8,512]{2,1,0:T(8,128)S(1)} fusion(f32[2,8,512,512]{2,3,1,0:T(8,128)} %get-tuple-element.82, f32[2,8,512]{2,1,0:T(8,128)S(1)} %get-tuple-element.81, pred[512,512]{0,1:T(8,128)(4,1)S(1)} %iota_compare_fusion), kind=kLoop, calls=%fused_computation.16 | loop fusion | flops 16769024 | bytes 17104896 | tf_op jit(solution)/shard_map/reduce_sum | solution.py:18
  42.2 0.0 all-to-all-done
  42.2 5.1 %all-to-all-start.1 = ((bf16[2,2,4,128,128]{4,3,1,0,2:T(8,128)(2,1)}), bf16[2,2,4,128,128]{4,3,1,0,2:T(8,128)(2,1)}, u32[]{:S(2)}, u32[]{:S(2)}) async-start(bf16[2,2,4,128,128]{4,3,1,0,2:T(8,128)(2,1)} %select_bitcast_fusion), calls=%async_computation.1 | async-start | bytes 1048576 | tf_op jit(solution)/shard_map/all_to_all | solution.py:107
  47.4 1.2 compare_and_fusion.2
  48.6 2.0 %select_bitcast_fusion.2 = bf16[2,2,4,128,128]{4,3,1,0,2:T(8,128)(2,1)} fusion(bf16[4,2,2,128,128]{4,3,2,1,0:T(8,128)(2,1)} %gather_fusion, pred[4]{0:T(512)(128)(4,1)S(1)} %get-tuple-element.86, pred[4]{0:T(512)(128)(4,1)S(1)} %get-tuple-element.85), kind=kLoop, calls=%fused_computation.47 | loop fusion | flops 524288 | bytes 1048584 | tf_op jit(solution)/shard_map/jit(_where)/select_n | solution.py:81
  50.6 1.9 %fusion.60 = (bf16[1,2,4,128,128]{4,3,1,0,2:T(8,128)(2,1)}, bf16[1,2,4,128,128]{4,3,1,0,2:T(8,128)(2,1)}) fusion(bf16[2,2,4,128,128]{4,3,1,0,2:T(8,128)(2,1)} %all-to-all-done), kind=kLoop, calls=%fused_computation.119 | loop fusion | bytes 1048576 | tf_op jit(solution)/shard_map/while/body/eval_jaxpr/slice | solution.py:41
  52.4 1.8 %copy.24 = bf16[1,2,4,128,128]{3,2,4,1,0:T(4,128)(2,1)} copy(bf16[1,2,4,128,128]{4,3,1,0,2:T(8,128)(2,1)} %get-tuple-element.72) | data formatting | bytes 524288 | tf_op jit(solution)/shard_map/while/body/eval_jaxpr/slice | solution.py:41
  54.3 1.8 %reshape.240 = bf16[2,512,128,1]{1,2,0,3:T(8,128)(2,1)} reshape(bf16[1,2,4,128,128]{3,2,4,1,0:T(4,128)(2,1)} %copy.24) | data formatting | bytes 524288 | tf_op jit(solution)/shard_map/while/body/eval_jaxpr/reshape;while/body/eval_jaxpr/squeeze | solution.py:41
  56.0 1.7 %copy.23 = bf16[1,2,4,128,128]{4,3,2,1,0:T(8,128)(2,1)} copy(bf16[1,2,4,128,128]{4,3,1,0,2:T(8,128)(2,1)} %get-tuple-element.73) | data formatting | bytes 524288 | tf_op jit(solution)/shard_map/while/body/eval_jaxpr/slice | solution.py:38
  57.7 3.7 %all-to-all-done.1 = bf16[2,2,4,128,128]{4,3,1,0,2:T(8,128)(2,1)} async-done(((bf16[2,2,4,128,128]{4,3,1,0,2:T(8,128)(2,1)}), bf16[2,2,4,128,128]{4,3,1,0,2:T(8,128)(2,1)}, u32[]{:S(2)}, u32[]{:S(2)}) %all-to-all-start.1) | async-done | bytes 524320 | tf_op jit(solution)/shard_map/all_to_all | solution.py:107
  61.4 4.3 %all-to-all-start.2 = ((bf16[2,2,4,128,128]{4,3,1,0,2:T(8,128)(2,1)}), bf16[2,2,4,128,128]{4,3,1,0,2:T(8,128)(2,1)}, u32[]{:S(2)}, u32[]{:S(2)}) async-start(bf16[2,2,4,128,128]{4,3,1,0,2:T(8,128)(2,1)} %select_bitcast_fusion.2), calls=%async_computation.2 | async-start | bytes 1048576 | tf_op jit(solution)/shard_map/all_to_all | solution.py:85
  65.7 1.9 %fusion.61 = (bf16[1,2,4,128,128]{4,3,1,0,2:T(8,128)(2,1)}, bf16[1,2,4,128,128]{4,3,1,0,2:T(8,128)(2,1)}) fusion(bf16[2,2,4,128,128]{4,3,1,0,2:T(8,128)(2,1)} %all-to-all-done.1), kind=kLoop, calls=%fused_computation.120 | loop fusion | bytes 1048576 | tf_op jit(solution)/shard_map/while/body/eval_jaxpr/slice | solution.py:41
  67.6 1.8 %copy.27 = bf16[1,2,4,128,128]{3,2,4,1,0:T(4,128)(2,1)} copy(bf16[1,2,4,128,128]{4,3,1,0,2:T(8,128)(2,1)} %get-tuple-element.74) | data formatting | bytes 524288 | tf_op jit(solution)/shard_map/while/body/eval_jaxpr/slice | solution.py:41
  69.4 1.8 %reshape.242 = bf16[2,512,128,1]{1,2,0,3:T(8,128)(2,1)} reshape(bf16[1,2,4,128,128]{3,2,4,1,0:T(4,128)(2,1)} %copy.27) | data formatting | bytes 524288 | tf_op jit(solution)/shard_map/while/body/eval_jaxpr/reshape;while/body/eval_jaxpr/squeeze | solution.py:41
  71.2 0.0 copy-start.4
  71.2 1.0 copy.26
  72.2 7.7 %bitcast_reduce_fusion = (f32[2,8,512]{2,1,0:T(8,128)S(1)}, f32[2,512,8,512]{3,1,2,0:T(8,128)}) fusion(pred[512]{0:T(512)(128)(4,1)S(1)} %broadcast_bitcast_fusion, bf16[2,512,128,1]{2,1,3,0:T(8,128)(2,1)S(1)} %bitcast.173, bf16[512,2,8,128]{3,2,1,0:T(8,128)(2,1)S(1)} %bitcast.167), kind=kOutput, calls=%fused_computation.6 | convolution fusion | flops 1086316544 | bytes 19169792 | tf_op jit(solution)/shard_map/while/body/eval_jaxpr/hgqd,hkd->hgqk/dot_general | solution.py:11
  79.8 0.0 copy-done.4
  79.8 0.0 copy-start.6
  79.8 2.7 %bitcast_reduce_fusion.1 = (f32[2,8,512]{2,1,0:T(8,128)S(1)}, f32[2,512,8,512]{3,1,2,0:T(8,128)S(1)}) fusion(pred[512]{0:T(512)(128)(4,1)S(1)} %broadcast_bitcast_fusion.1, bf16[2,512,128,1]{2,1,3,0:T(8,128)(2,1)S(1)} %bitcast.172, bf16[512,2,8,128]{3,2,1,0:T(8,128)(2,1)S(1)} %bitcast.168), kind=kOutput, calls=%fused_computation.9 | convolution fusion | flops 1086316544 | bytes 19169792 | tf_op jit(solution)/shard_map/while/body/eval_jaxpr/hgqd,hkd->hgqk/dot_general | solution.py:11
  82.6 7.9 %fusion.7 = f32[2,8,512]{2,1,0:T(8,128)S(1)} fusion(f32[2,512,8,512]{3,1,2,0:T(8,128)} %get-tuple-element.80, f32[2,8,512]{2,1,0:T(8,128)S(1)} %get-tuple-element.57, pred[512]{0:T(512)(128)(4,1)S(1)} %broadcast_bitcast_fusion), kind=kLoop, calls=%fused_computation.20 | loop fusion | flops 16769024 | bytes 16843264 | tf_op jit(solution)/shard_map/while/body/eval_jaxpr/reduce_sum | solution.py:18
  90.5 0.0 copy-done.6
  90.5 0.0 copy-start.5
  90.5 8.0 %fusion.9 = f32[2,8,512,128]{2,3,1,0:T(8,128)S(1)} fusion(f32[2,512,8,512]{3,1,2,0:T(8,128)} %get-tuple-element.80, f32[2,8,512]{2,1,0:T(8,128)S(1)} %get-tuple-element.57, pred[512]{0:T(512)(128)(4,1)S(1)} %broadcast_bitcast_fusion, bf16[2,512,128,1]{1,2,0,3:T(8,128)(2,1)S(1)} %copy-done.6), kind=kOutput, calls=%fused_computation.22 | convolution fusion | flops 1090519040 | bytes 21266944 | tf_op jit(solution)/shard_map/while/body/eval_jaxpr/hgqk,hkd->hgqd/dot_general | solution.py:19
  98.5 0.0 copy-start.3
  98.5 3.8 %fusion.5 = f32[2,8,512]{2,1,0:T(8,128)S(1)} fusion(f32[2,512,8,512]{3,1,2,0:T(8,128)S(1)} %get-tuple-element.84, f32[2,8,512]{2,1,0:T(8,128)S(1)} %get-tuple-element.58, pred[512]{0:T(512)(128)(4,1)S(1)} %broadcast_bitcast_fusion.1), kind=kLoop, calls=%fused_computation.18 | loop fusion | flops 16769024 | bytes 16843264 | tf_op jit(solution)/shard_map/while/body/eval_jaxpr/reduce_sum | solution.py:18
  102.3 0.0 copy-done.5
  102.3 5.5 %fusion.11 = f32[2,8,512,128]{2,3,1,0:T(8,128)} fusion(f32[2,512,8,512]{3,1,2,0:T(8,128)S(1)} %get-tuple-element.84, f32[2,8,512]{2,1,0:T(8,128)S(1)} %get-tuple-element.58, pred[512]{0:T(512)(128)(4,1)S(1)} %broadcast_bitcast_fusion.1, bf16[2,512,128,1]{1,2,0,3:T(8,128)(2,1)S(1)} %copy-done.5), kind=kOutput, calls=%fused_computation.23 | convolution fusion | flops 1090519040 | bytes 21266944 | tf_op jit(solution)/shard_map/while/body/eval_jaxpr/hgqk,hkd->hgqd/dot_general | solution.py:19
  107.8 0.0 copy-start.1
  107.9 0.0 copy-done.3
  107.9 9.7 %fusion.19 = bf16[512,2,8,128]{0,3,2,1:T(8,128)(2,1)S(1)} fusion(f32[2,8,512,128]{2,3,1,0:T(8,128)S(1)} %fusion.9, f32[2,8,512,128]{2,3,1,0:T(8,128)} %fusion.11, f32[2,8,512,512]{2,3,1,0:T(8,128)} %get-tuple-element.82, f32[2,8,512]{2,1,0:T(8,128)S(1)} %get-tuple-element.81, pred[512,512]{0,1:T(8,128)(4,1)S(1)} %iota_compare_fusion, ...), kind=kOutput, calls=%fused_computation.30 | convolution fusion | flops 1097859072 | bytes 27951104 | tf_op jit(solution)/shard_map/hgqk,hkd->hgqd/dot_general | solution.py:19
  117.6 2.4 %copy.29 = bf16[512,2048]{1,0:T(8,128)(2,1)} copy(bf16[512,2048]{0,1:T(8,128)(2,1)S(1)} %bitcast.170) | data formatting | bytes 4194304
  120.0 0.0 all-to-all-done.2
  120.0 1.8 %scatter_fusion = bf16[2,2,8,128,128]{4,3,2,1,0:T(8,128)(2,1)S(1)} fusion(bf16[2,2,8,128,128]{4,3,2,1,0:T(8,128)(2,1)S(1)} %copy.61, s32[4]{0:T(128)S(1)} %compare_select_fusion.4, bf16[4,2,2,128,128]{4,3,2,1,0:T(8,128)(2,1)} %bitcast.42), kind=kCustom, calls=%fused_computation.4 | custom fusion | bytes 1572880 | tf_op jit(solution)/shard_map/scatter | solution.py:130
  121.8 0.0 copy-start.2
  121.8 1.0 copy-done.2
  122.8 0.0 copy-done.1
  (10 shorter events, 0.1 us)
Async XLA Ops:
  0.6 1.3 %copy-start = (s32[4,4,2]{1,2,0:T(2,128)S(1)}, s32[4,4,2]{1,2,0:T(2,128)}, u32[]{:S(2)}) copy-start(s32[4,4,2]{1,2,0:T(2,128)} %param.13) | copy-start | bytes 388
  3.6 38.6 %all-to-all-start = ((bf16[2,2,4,128,128]{4,3,1,0,2:T(8,128)(2,1)}), bf16[2,2,4,128,128]{4,3,1,0,2:T(8,128)(2,1)}, u32[]{:S(2)}, u32[]{:S(2)}) async-start(bf16[2,2,4,128,128]{4,3,1,0,2:T(8,128)(2,1)} %select_bitcast_fusion.1), calls=%async_computation | async-start | bytes 1048576 | tf_op jit(solution)/shard_map/all_to_all | solution.py:84
  42.2 19.1 %all-to-all-start.1 = ((bf16[2,2,4,128,128]{4,3,1,0,2:T(8,128)(2,1)}), bf16[2,2,4,128,128]{4,3,1,0,2:T(8,128)(2,1)}, u32[]{:S(2)}, u32[]{:S(2)}) async-start(bf16[2,2,4,128,128]{4,3,1,0,2:T(8,128)(2,1)} %select_bitcast_fusion), calls=%async_computation.1 | async-start | bytes 1048576 | tf_op jit(solution)/shard_map/all_to_all | solution.py:107
  61.4 58.6 %all-to-all-start.2 = ((bf16[2,2,4,128,128]{4,3,1,0,2:T(8,128)(2,1)}), bf16[2,2,4,128,128]{4,3,1,0,2:T(8,128)(2,1)}, u32[]{:S(2)}, u32[]{:S(2)}) async-start(bf16[2,2,4,128,128]{4,3,1,0,2:T(8,128)(2,1)} %select_bitcast_fusion.2), calls=%async_computation.2 | async-start | bytes 1048576 | tf_op jit(solution)/shard_map/all_to_all | solution.py:85
  71.2 8.7 %copy-start.4 = (bf16[1,2,4,128,128]{4,3,2,1,0:T(8,128)(2,1)S(1)}, bf16[1,2,4,128,128]{4,3,2,1,0:T(8,128)(2,1)}, u32[]{:S(2)}) copy-start(bf16[1,2,4,128,128]{4,3,2,1,0:T(8,128)(2,1)} %copy.23) | copy-start | bytes 786436
  79.8 10.7 %copy-start.6 = (bf16[2,512,128,1]{1,2,0,3:T(8,128)(2,1)S(1)}, bf16[2,512,128,1]{1,2,0,3:T(8,128)(2,1)}, u32[]{:S(2)}) copy-start(bf16[2,512,128,1]{1,2,0,3:T(8,128)(2,1)} %reshape.242) | copy-start | bytes 786436
  90.5 11.8 %copy-start.5 = (bf16[2,512,128,1]{1,2,0,3:T(8,128)(2,1)S(1)}, bf16[2,512,128,1]{1,2,0,3:T(8,128)(2,1)}, u32[]{:S(2)}) copy-start(bf16[2,512,128,1]{1,2,0,3:T(8,128)(2,1)} %reshape.240) | copy-start | bytes 786436
  98.5 9.4 %copy-start.3 = (bf16[2,2,512,128]{3,2,1,0:T(8,128)(2,1)S(1)}, bf16[2,2,512,128]{3,2,1,0:T(8,128)(2,1)}, u32[]{:S(2)}) copy-start(bf16[2,2,512,128]{3,2,1,0:T(8,128)(2,1)} %param.9) | copy-start | bytes 1572868
  107.8 14.9 %copy-start.1 = (s32[4,4,2]{1,2,0:T(2,128)S(1)}, s32[4,4,2]{1,2,0:T(2,128)}, u32[]{:S(2)}) copy-start(s32[4,4,2]{1,2,0:T(2,128)} %param.13) | copy-start | bytes 388
  121.8 1.0 copy-start.2
where the time goes:
time: 124 us; the launch traced here: 123 us
  matrix products  41.8 us (34%)
  other arithmetic  30.5 us (25%)
  local copies, waits for them, and re-layouts  30.1 us (24%)
  starting transfers between devices  15.8 us (13%)
  waiting for transfers between devices  3.71 us (3%)
    dot_general x3, matrix products, attend_block(): jnp.einsum('hgqk,hkd->hgqd', weights.astype(jnp.bfloat16), value_rows, pr...  23.2 us
    reduce_sum x3, other arithmetic, attend_block(): weight_sum = weight_sum * factor + jnp.sum(weights, axis=-1)  21.1 us
    dot_general x3, matrix products, attend_block(): jnp.einsum('hgqd,hkd->hgqk', query_heads, key_rows, preferred_element_typ...  18.6 us
    slice x4, local copies, waits for them, and re-layouts, block_step(): block_pages[1]  7.37 us
    unnamed x18, local copies, waits for them, and re-layouts  6.81 us
    all_to_all x1, starting transfers between devices, body(): lax.all_to_all(first_send, 'pool', split_axis=2, concat_axis=2, tiled=True)  6.35 us
    all_to_all x1, starting transfers between devices, body(): lax.all_to_all(level_rows(begin_level, end_level), 'pool', split_axis=2,...  5.11 us
    all_to_all x1, starting transfers between devices, body(): lax.all_to_all(back_send, 'pool', split_axis=2, concat_axis=2, tiled=True)  4.32 us
  transfers between devices with their start and end apart: 3, of which 1 were waited for; matrix products, arithmetic and copies ran while one was open for 79% of the time, Pallas kernels for 0%

commit v1 on v0

--- a/solution.py
+++ b/solution.py
@@ -81,7 +81,12 @@
     back_send = jnp.where(wanted[None, None, :, None, None], picked, jnp.zeros_like(picked))
     level_spans = [(level_one, level_one + 1) for level_one in range(levels)]
     first_send = level_rows(level_spans[0][0], level_spans[0][1])
-    first_recv = lax.all_to_all(first_send, "pool", split_axis=2, concat_axis=2, tiled=True)
+    first_recv = jnp.concatenate(
+        lax.all_to_all(
+            jnp.stack(jnp.split(first_send, lax.axis_size("pool"), axis=2)), "pool", 0, 0
+        ),
+        axis=2,
+    )
     returned = lax.all_to_all(back_send, "pool", split_axis=2, concat_axis=2, tiled=True)
     query_heads = jnp.transpose(
         queries.reshape(suffix, local_heads, per_kv, head_dim), (1, 2, 0, 3)

time: 124 us -> 124 us (level)
  no operation moved by 1% of the time
where the time goes in v1:
time: 124 us; the launch traced here: 123 us
  matrix products  41.8 us (34%)
  other arithmetic  30.7 us (25%)
  local copies, waits for them, and re-layouts  30.2 us (24%)
  starting transfers between devices  15.8 us (13%)
  waiting for transfers between devices  3.66 us (3%)
    dot_general x3, matrix products, attend_block(): jnp.einsum('hgqk,hkd->hgqd', weights.astype(jnp.bfloat16), value_rows, pr...  23.2 us
    reduce_sum x3, other arithmetic, attend_block(): weight_sum = weight_sum * factor + jnp.sum(weights, axis=-1)  21.1 us
    dot_general x3, matrix products, attend_block(): jnp.einsum('hgqd,hkd->hgqk', query_heads, key_rows, preferred_element_typ...  18.6 us
    slice x4, local copies, waits for them, and re-layouts, block_step(): block_pages[1]  7.37 us
    unnamed x18, local copies, waits for them, and re-layouts  6.81 us
    all_to_all x1, starting transfers between devices, body(): lax.all_to_all(jnp.stack(jnp.split(first_send, lax.axis_size('pool'), axi...  6.35 us
    all_to_all x1, starting transfers between devices, body(): lax.all_to_all(level_rows(begin_level, end_level), 'pool', split_axis=2,...  5.11 us
    all_to_all x1, starting transfers between devices, body(): lax.all_to_all(back_send, 'pool', split_axis=2, concat_axis=2, tiled=True)  4.31 us
  transfers between devices with their start and end apart: 3, of which 1 were waited for; matrix products, arithmetic and copies ran while one was open for 79% of the time, Pallas kernels for 0%

profile of v1, /device:TPU:0, one launch (start us, length us, event | category | flops | bytes accessed | tf_op | source)
XLA Modules:
  0.0 123.1 jit_solution(14236600993438357906)
XLA Ops:
  0.6 0.0 copy-start
  0.6 1.2 %copy.61 = bf16[2,2,8,128,128]{4,3,2,1,0:T(8,128)(2,1)S(1)} copy(bf16[2,2,8,128,128]{4,3,2,1,0:T(8,128)(2,1)} %param.10) | data formatting | bytes 2097152
  1.9 0.0 copy-done
  1.9 0.1 constant_dynamic-slice_fusion
  2.0 0.1 copy.22
  2.1 0.6 gather_fusion.2
  2.7 0.1 select_bitcast_fusion.1
  2.9 0.9 pad_maximum_fusion
  3.8 6.3 %all-to-all-start = ((bf16[4,2,2,1,128,128]{5,4,2,1,3,0:T(8,128)(2,1)}), bf16[4,2,2,1,128,128]{5,4,2,1,3,0:T(8,128)(2,1)}, u32[]{:S(2)}, u32[]{:S(2)}) async-start(bf16[4,2,2,1,128,128]{5,4,2,1,3,0:T(8,128)(2,1)} %pad_maximum_fusion), calls=%async_computation | async-start | bytes 1048576 | tf_op jit(solution)/shard_map/all_to_all | solution.py:85
  10.1 1.3 %dynamic_slice.17 = s32[1]{0:T(128)} dynamic-slice(s32[4]{0:T(128)} %param.12, s32[]{:T(128)S(6)} %select_n.118), dynamic_slice_sizes={1} | dynamic-slice | bytes 12 | tf_op jit(solution)/shard_map/dynamic_slice | solution.py:64
  11.4 1.3 %dynamic_slice.18 = s32[1]{0:T(128)} dynamic-slice(s32[4]{0:T(128)} %param.11, s32[]{:T(128)S(6)} %select_n.118), dynamic_slice_sizes={1} | dynamic-slice | bytes 12 | tf_op jit(solution)/shard_map/dynamic_slice | solution.py:63
  12.7 0.7 compare_select_fusion.5
  13.4 1.3 %fusion.50 = s32[4]{0:T(128)S(1)} fusion(s32[]{:T(128)} %bitcast.10, s32[]{:T(128)} %bitcast.9), kind=kLoop, calls=%fused_computation.110 | loop fusion | flops 68 | bytes 24 | tf_op jit(solution)/shard_map/jit(_take)/jit(_where)/select_n | solution.py:80
  14.6 1.3 %add_compare_fusion = (pred[4]{0:T(512)(128)(4,1)S(1)}, pred[4]{0:T(512)(128)(4,1)S(1)}) fusion(s32[]{:T(128)} %bitcast.10, s32[]{:T(128)} %bitcast.9), kind=kLoop, calls=%fused_computation.112 | loop fusion | flops 60 | bytes 16 | tf_op jit(solution)/shard_map/while/body/eval_jaxpr/lt | solution.py:44
  15.9 0.1 iota_compare_fusion
  16.0 0.1 broadcast_bitcast_fusion
  16.1 0.1 broadcast_bitcast_fusion.1
  16.2 0.6 gather_fusion.1
  16.8 1.4 %gather_fusion.3 = bf16[4,2,2,128,128]{4,3,2,1,0:T(8,128)(2,1)} fusion(bf16[2,2,8,128,128]{4,3,2,1,0:T(8,128)(2,1)S(1)} %copy.61, s32[1024]{0:T(1024)S(1)} %pad_clamp_fusion.1), kind=kCustom, calls=%fused_computation.1.clone | custom fusion | bytes 1048592 | tf_op jit(solution)/shard_map/jit(_take)/gather | solution.py:70
  18.2 2.2 %copy.40 = bf16[64,8,16,128]{3,2,1,0:T(8,128)(2,1)S(1)} copy(bf16[64,8,16,128]{3,1,2,0:T(8,128)(2,1)} %bitcast.178) | data formatting | bytes 4194304
  20.4 2.5 %gather_fusion = bf16[4,2,2,128,128]{4,3,2,1,0:T(8,128)(2,1)} fusion(bf16[2,2,4,128,128]{4,3,2,1,0:T(8,128)(2,1)} %bitcast.180, s32[1024]{0:T(1024)S(1)} %pad_clamp_fusion), kind=kCustom, calls=%fused_computation.2 | custom fusion | bytes 1048592 | tf_op jit(solution)/shard_map/jit(_take)/gather | solution.py:80
  22.9 1.9 %select_bitcast_fusion = bf16[2,2,4,128,128]{4,3,1,0,2:T(8,128)(2,1)} fusion(bf16[4,2,2,128,128]{4,3,2,1,0:T(8,128)(2,1)} %gather_fusion.3, pred[4]{0:T(512)(128)(4,1)S(1)} %get-tuple-element.81), kind=kLoop, calls=%fused_computation.46 | loop fusion | flops 262144 | bytes 1048580 | tf_op jit(solution)/shard_map/jit(_take)/select_n | solution.py:70
  24.9 8.3 %fusion.2 = (f32[2,8,512]{2,1,0:T(8,128)S(1)}, f32[2,8,512,512]{2,3,1,0:T(8,128)}) fusion(pred[512,512]{0,1:T(8,128)(4,1)S(1)} %iota_compare_fusion, bf16[2,2,512,128]{3,2,1,0:T(8,128)(2,1)} %param.9, bf16[512,2,8,128]{3,2,1,0:T(8,128)(2,1)S(1)} %bitcast.175), kind=kOutput, calls=%fused_computation.15 | convolution fusion | flops 1086316544 | bytes 19431424 | tf_op jit(solution)/shard_map/hgqd,hkd->hgqk/dot_general | solution.py:11
  33.1 9.4 %fusion.3 = f32[2,8,512]{2,1,0:T(8,128)S(1)} fusion(f32[2,8,512,512]{2,3,1,0:T(8,128)} %get-tuple-element.86, f32[2,8,512]{2,1,0:T(8,128)S(1)} %get-tuple-element.85, pred[512,512]{0,1:T(8,128)(4,1)S(1)} %iota_compare_fusion), kind=kLoop, calls=%fused_computation.16 | loop fusion | flops 16769024 | bytes 17104896 | tf_op jit(solution)/shard_map/reduce_sum | solution.py:18
  42.5 0.0 all-to-all-done
  42.6 5.1 %all-to-all-start.1 = ((bf16[2,2,4,128,128]{4,3,1,0,2:T(8,128)(2,1)}), bf16[2,2,4,128,128]{4,3,1,0,2:T(8,128)(2,1)}, u32[]{:S(2)}, u32[]{:S(2)}) async-start(bf16[2,2,4,128,128]{4,3,1,0,2:T(8,128)(2,1)} %select_bitcast_fusion), calls=%async_computation.1 | async-start | bytes 1048576 | tf_op jit(solution)/shard_map/all_to_all | solution.py:112
  47.7 1.3 %compare_and_fusion.2 = (pred[4]{0:T(512)(128)(4,1)S(1)}, pred[4]{0:T(512)(128)(4,1)S(1)}) fusion(s32[]{:T(128)} %bitcast.10, s32[]{:T(128)} %bitcast.9), kind=kLoop, calls=%fused_computation.92 | loop fusion | flops 84 | bytes 16 | tf_op jit(solution)/shard_map/jit(_take)/and | solution.py:80
  49.0 2.0 %select_bitcast_fusion.2 = bf16[2,2,4,128,128]{4,3,1,0,2:T(8,128)(2,1)} fusion(bf16[4,2,2,128,128]{4,3,2,1,0:T(8,128)(2,1)} %gather_fusion, pred[4]{0:T(512)(128)(4,1)S(1)} %get-tuple-element.90, pred[4]{0:T(512)(128)(4,1)S(1)} %get-tuple-element.89), kind=kLoop, calls=%fused_computation.48 | loop fusion | flops 524288 | bytes 1048584 | tf_op jit(solution)/shard_map/jit(_where)/select_n | solution.py:81
  50.9 1.9 %fusion.60 = (bf16[1,2,4,1,128,128]{5,4,1,0,3,2:T(8,128)(2,1)}, bf16[1,2,4,1,128,128]{5,4,1,0,3,2:T(8,128)(2,1)}) fusion(bf16[2,2,4,1,128,128]{5,4,1,0,3,2:T(8,128)(2,1)} %bitcast.19), kind=kLoop, calls=%fused_computation.124 | loop fusion | bytes 1048576 | tf_op jit(solution)/shard_map/while/body/eval_jaxpr/slice | solution.py:41
  52.8 1.8 %copy.24 = bf16[1,2,4,1,128,128]{4,2,5,1,3,0:T(4,128)(2,1)} copy(bf16[1,2,4,1,128,128]{5,4,1,0,3,2:T(8,128)(2,1)} %get-tuple-element.72) | data formatting | bytes 524288 | tf_op jit(solution)/shard_map/while/body/eval_jaxpr/slice | solution.py:41
  54.6 1.8 %reshape.249 = bf16[2,512,128,1]{1,2,0,3:T(8,128)(2,1)} reshape(bf16[1,2,4,1,128,128]{4,2,5,1,3,0:T(4,128)(2,1)} %copy.24) | data formatting | bytes 524288 | tf_op jit(solution)/shard_map/while/body/eval_jaxpr/reshape;while/body/eval_jaxpr/squeeze | solution.py:41
  56.4 1.7 %copy.23 = bf16[1,2,4,1,128,128]{5,4,2,1,3,0:T(8,128)(2,1)} copy(bf16[1,2,4,1,128,128]{5,4,1,0,3,2:T(8,128)(2,1)} %get-tuple-element.73) | data formatting | bytes 524288 | tf_op jit(solution)/shard_map/while/body/eval_jaxpr/slice | solution.py:38
  58.0 3.7 %all-to-all-done.1 = bf16[2,2,4,128,128]{4,3,1,0,2:T(8,128)(2,1)} async-done(((bf16[2,2,4,128,128]{4,3,1,0,2:T(8,128)(2,1)}), bf16[2,2,4,128,128]{4,3,1,0,2:T(8,128)(2,1)}, u32[]{:S(2)}, u32[]{:S(2)}) %all-to-all-start.1) | async-done | bytes 524320 | tf_op jit(solution)/shard_map/all_to_all | solution.py:112
  61.7 4.3 %all-to-all-start.2 = ((bf16[2,2,4,128,128]{4,3,1,0,2:T(8,128)(2,1)}), bf16[2,2,4,128,128]{4,3,1,0,2:T(8,128)(2,1)}, u32[]{:S(2)}, u32[]{:S(2)}) async-start(bf16[2,2,4,128,128]{4,3,1,0,2:T(8,128)(2,1)} %select_bitcast_fusion.2), calls=%async_computation.2 | async-start | bytes 1048576 | tf_op jit(solution)/shard_map/all_to_all | solution.py:90
  66.0 1.9 %fusion.61 = (bf16[1,2,4,128,128]{4,3,1,0,2:T(8,128)(2,1)}, bf16[1,2,4,128,128]{4,3,1,0,2:T(8,128)(2,1)}) fusion(bf16[2,2,4,128,128]{4,3,1,0,2:T(8,128)(2,1)} %all-to-all-done.1), kind=kLoop, calls=%fused_computation.125 | loop fusion | bytes 1048576 | tf_op jit(solution)/shard_map/while/body/eval_jaxpr/slice | solution.py:41
  67.9 1.8 %copy.27 = bf16[1,2,4,128,128]{3,2,4,1,0:T(4,128)(2,1)} copy(bf16[1,2,4,128,128]{4,3,1,0,2:T(8,128)(2,1)} %get-tuple-element.74) | data formatting | bytes 524288 | tf_op jit(solution)/shard_map/while/body/eval_jaxpr/slice | solution.py:41
  69.7 1.8 %reshape.251 = bf16[2,512,128,1]{1,2,0,3:T(8,128)(2,1)} reshape(bf16[1,2,4,128,128]{3,2,4,1,0:T(4,128)(2,1)} %copy.27) | data formatting | bytes 524288 | tf_op jit(solution)/shard_map/while/body/eval_jaxpr/reshape;while/body/eval_jaxpr/squeeze | solution.py:41
  71.5 0.0 copy-start.4
  71.5 1.0 copy.26
  72.5 7.6 %bitcast_reduce_fusion = (f32[2,8,512]{2,1,0:T(8,128)S(1)}, f32[2,512,8,512]{3,1,2,0:T(8,128)}) fusion(pred[512]{0:T(512)(128)(4,1)S(1)} %broadcast_bitcast_fusion, bf16[2,512,128,1]{2,1,3,0:T(8,128)(2,1)S(1)} %bitcast.182, bf16[512,2,8,128]{3,2,1,0:T(8,128)(2,1)S(1)} %bitcast.176), kind=kOutput, calls=%fused_computation.6 | convolution fusion | flops 1086316544 | bytes 19169792 | tf_op jit(solution)/shard_map/while/body/eval_jaxpr/hgqd,hkd->hgqk/dot_general | solution.py:11
  80.1 0.0 copy-done.4
  80.1 0.0 copy-start.6
  80.1 2.7 %bitcast_reduce_fusion.1 = (f32[2,8,512]{2,1,0:T(8,128)S(1)}, f32[2,512,8,512]{3,1,2,0:T(8,128)S(1)}) fusion(pred[512]{0:T(512)(128)(4,1)S(1)} %broadcast_bitcast_fusion.1, bf16[2,512,128,1]{2,1,3,0:T(8,128)(2,1)S(1)} %bitcast.181, bf16[512,2,8,128]{3,2,1,0:T(8,128)(2,1)S(1)} %bitcast.177), kind=kOutput, calls=%fused_computation.9 | convolution fusion | flops 1086316544 | bytes 19169792 | tf_op jit(solution)/shard_map/while/body/eval_jaxpr/hgqd,hkd->hgqk/dot_general | solution.py:11
  82.9 7.9 %fusion.7 = f32[2,8,512]{2,1,0:T(8,128)S(1)} fusion(f32[2,512,8,512]{3,1,2,0:T(8,128)} %get-tuple-element.84, f32[2,8,512]{2,1,0:T(8,128)S(1)} %get-tuple-element.57, pred[512]{0:T(512)(128)(4,1)S(1)} %broadcast_bitcast_fusion), kind=kLoop, calls=%fused_computation.20 | loop fusion | flops 16769024 | bytes 16843264 | tf_op jit(solution)/shard_map/while/body/eval_jaxpr/reduce_sum | solution.py:18
  90.8 0.0 copy-done.6
  90.8 0.0 copy-start.5
  90.8 8.0 %fusion.9 = f32[2,8,512,128]{2,3,1,0:T(8,128)S(1)} fusion(f32[2,512,8,512]{3,1,2,0:T(8,128)} %get-tuple-element.84, f32[2,8,512]{2,1,0:T(8,128)S(1)} %get-tuple-element.57, pred[512]{0:T(512)(128)(4,1)S(1)} %broadcast_bitcast_fusion, bf16[2,512,128,1]{1,2,0,3:T(8,128)(2,1)S(1)} %copy-done.6), kind=kOutput, calls=%fused_computation.22 | convolution fusion | flops 1090519040 | bytes 21266944 | tf_op jit(solution)/shard_map/while/body/eval_jaxpr/hgqk,hkd->hgqd/dot_general | solution.py:19
  98.8 0.0 copy-start.3
  98.8 3.8 %fusion.5 = f32[2,8,512]{2,1,0:T(8,128)S(1)} fusion(f32[2,512,8,512]{3,1,2,0:T(8,128)S(1)} %get-tuple-element.88, f32[2,8,512]{2,1,0:T(8,128)S(1)} %get-tuple-element.58, pred[512]{0:T(512)(128)(4,1)S(1)} %broadcast_bitcast_fusion.1), kind=kLoop, calls=%fused_computation.18 | loop fusion | flops 16769024 | bytes 16843264 | tf_op jit(solution)/shard_map/while/body/eval_jaxpr/reduce_sum | solution.py:18
  102.6 0.0 copy-done.5
  102.6 5.5 %fusion.11 = f32[2,8,512,128]{2,3,1,0:T(8,128)} fusion(f32[2,512,8,512]{3,1,2,0:T(8,128)S(1)} %get-tuple-element.88, f32[2,8,512]{2,1,0:T(8,128)S(1)} %get-tuple-element.58, pred[512]{0:T(512)(128)(4,1)S(1)} %broadcast_bitcast_fusion.1, bf16[2,512,128,1]{1,2,0,3:T(8,128)(2,1)S(1)} %copy-done.5), kind=kOutput, calls=%fused_computation.23 | convolution fusion | flops 1090519040 | bytes 21266944 | tf_op jit(solution)/shard_map/while/body/eval_jaxpr/hgqk,hkd->hgqd/dot_general | solution.py:19
  108.1 0.0 copy-start.1
  108.2 0.0 copy-done.3
  108.2 9.7 %fusion.19 = bf16[512,2,8,128]{0,3,2,1:T(8,128)(2,1)S(1)} fusion(f32[2,8,512,128]{2,3,1,0:T(8,128)S(1)} %fusion.9, f32[2,8,512,128]{2,3,1,0:T(8,128)} %fusion.11, f32[2,8,512,512]{2,3,1,0:T(8,128)} %get-tuple-element.86, f32[2,8,512]{2,1,0:T(8,128)S(1)} %get-tuple-element.85, pred[512,512]{0,1:T(8,128)(4,1)S(1)} %iota_compare_fusion, ...), kind=kOutput, calls=%fused_computation.30 | convolution fusion | flops 1097859072 | bytes 27951104 | tf_op jit(solution)/shard_map/hgqk,hkd->hgqd/dot_general | solution.py:19
  117.9 2.4 %copy.29 = bf16[512,2048]{1,0:T(8,128)(2,1)} copy(bf16[512,2048]{0,1:T(8,128)(2,1)S(1)} %bitcast.179) | data formatting | bytes 4194304
  120.3 0.0 all-to-all-done.2
  120.3 1.8 %scatter_fusion = bf16[2,2,8,128,128]{4,3,2,1,0:T(8,128)(2,1)S(1)} fusion(bf16[2,2,8,128,128]{4,3,2,1,0:T(8,128)(2,1)S(1)} %copy.61, s32[4]{0:T(128)S(1)} %compare_select_fusion.4, bf16[4,2,2,128,128]{4,3,2,1,0:T(8,128)(2,1)} %bitcast.47), kind=kCustom, calls=%fused_computation.4 | custom fusion | bytes 1572880 | tf_op jit(solution)/shard_map/scatter | solution.py:135
  122.1 0.0 copy-start.2
  122.1 1.0 copy-done.2
  123.1 0.0 copy-done.1
  (11 shorter events, 0.1 us)
Async XLA Ops:
  0.6 1.3 %copy-start = (s32[4,4,2]{1,2,0:T(2,128)S(1)}, s32[4,4,2]{1,2,0:T(2,128)}, u32[]{:S(2)}) copy-start(s32[4,4,2]{1,2,0:T(2,128)} %param.13) | copy-start | bytes 388
  3.8 38.8 %all-to-all-start = ((bf16[4,2,2,1,128,128]{5,4,2,1,3,0:T(8,128)(2,1)}), bf16[4,2,2,1,128,128]{5,4,2,1,3,0:T(8,128)(2,1)}, u32[]{:S(2)}, u32[]{:S(2)}) async-start(bf16[4,2,2,1,128,128]{5,4,2,1,3,0:T(8,128)(2,1)} %pad_maximum_fusion), calls=%async_computation | async-start | bytes 1048576 | tf_op jit(solution)/shard_map/all_to_all | solution.py:85
  42.6 19.1 %all-to-all-start.1 = ((bf16[2,2,4,128,128]{4,3,1,0,2:T(8,128)(2,1)}), bf16[2,2,4,128,128]{4,3,1,0,2:T(8,128)(2,1)}, u32[]{:S(2)}, u32[]{:S(2)}) async-start(bf16[2,2,4,128,128]{4,3,1,0,2:T(8,128)(2,1)} %select_bitcast_fusion), calls=%async_computation.1 | async-start | bytes 1048576 | tf_op jit(solution)/shard_map/all_to_all | solution.py:112
  61.7 58.6 %all-to-all-start.2 = ((bf16[2,2,4,128,128]{4,3,1,0,2:T(8,128)(2,1)}), bf16[2,2,4,128,128]{4,3,1,0,2:T(8,128)(2,1)}, u32[]{:S(2)}, u32[]{:S(2)}) async-start(bf16[2,2,4,128,128]{4,3,1,0,2:T(8,128)(2,1)} %select_bitcast_fusion.2), calls=%async_computation.2 | async-start | bytes 1048576 | tf_op jit(solution)/shard_map/all_to_all | solution.py:90
  71.5 8.7 %copy-start.4 = (bf16[1,2,4,1,128,128]{5,4,2,1,3,0:T(8,128)(2,1)S(1)}, bf16[1,2,4,1,128,128]{5,4,2,1,3,0:T(8,128)(2,1)}, u32[]{:S(2)}) copy-start(bf16[1,2,4,1,128,128]{5,4,2,1,3,0:T(8,128)(2,1)} %copy.23) | copy-start | bytes 786436
  80.1 10.7 %copy-start.6 = (bf16[2,512,128,1]{1,2,0,3:T(8,128)(2,1)S(1)}, bf16[2,512,128,1]{1,2,0,3:T(8,128)(2,1)}, u32[]{:S(2)}) copy-start(bf16[2,512,128,1]{1,2,0,3:T(8,128)(2,1)} %reshape.251) | copy-start | bytes 786436
  90.8 11.8 %copy-start.5 = (bf16[2,512,128,1]{1,2,0,3:T(8,128)(2,1)S(1)}, bf16[2,512,128,1]{1,2,0,3:T(8,128)(2,1)}, u32[]{:S(2)}) copy-start(bf16[2,512,128,1]{1,2,0,3:T(8,128)(2,1)} %reshape.249) | copy-start | bytes 786436
  98.8 9.4 %copy-start.3 = (bf16[2,2,512,128]{3,2,1,0:T(8,128)(2,1)S(1)}, bf16[2,2,512,128]{3,2,1,0:T(8,128)(2,1)}, u32[]{:S(2)}) copy-start(bf16[2,2,512,128]{3,2,1,0:T(8,128)(2,1)} %param.9) | copy-start | bytes 1572868
  108.1 14.9 %copy-start.1 = (s32[4,4,2]{1,2,0:T(2,128)S(1)}, s32[4,4,2]{1,2,0:T(2,128)}, u32[]{:S(2)}) copy-start(s32[4,4,2]{1,2,0:T(2,128)} %param.13) | copy-start | bytes 388
  122.1 1.0 copy-start.2
